TPU v7x, 256 devices: a whole 4x4x8 slice. The times are simulated.
256 devices in a mesh: leaf: 16 (over y, x), row: 16 (over z, core).
Axes of the slice: x: 4, y: 4, z: 8, core: 2. Of those that a mesh axis runs over, the one named last changes fastest.
Arguments:
- sigma_root: float32 [2048, 2048], P(None, 'row')
- linv_one: bfloat16 [16, 2048, 2048], P('leaf', None, 'row'), as said below
- panel_one: bfloat16 [16, 512, 2048], P('leaf', None, 'row'), may hold values from -1.25 to 1.25
- tiles_one: int32 [16, 4], replicated, may hold values from 0 to 15, as said below
- mask_one: int32 [16, 4, 16], P('leaf', None, 'row'), may hold values 0 or 1
- linv_two: bfloat16 [16, 2048, 2048], P('leaf', None, 'row'), as said below
- panel_two: bfloat16 [16, 512, 2048], P('leaf', None, 'row'), may hold values from -1.25 to 1.25
- tiles_two: int32 [16, 4], replicated, may hold values from 0 to 15, as said below
- mask_two: int32 [16, 4, 16], P('leaf', None, 'row'), may hold values 0 or 1
- parent: int32 [16], replicated, may hold values from 0 to 15
Outputs:
- sigma_one: float32 [16, 2048, 2048], P('leaf', None, 'row')
- cross_one: float32 [16, 512, 2048], P('leaf', None, 'row')
- sigma_two: float32 [16, 2048, 2048], P('leaf', None, 'row')
- cross_two: float32 [16, 512, 2048], P('leaf', None, 'row')
Inputs may be any that keep to these rules, and one draw needn't show every extreme that they name: `tiles_one`: each row holds 4 different tile numbers in increasing order. `tiles_two`: each row holds 4 different tile numbers in increasing order. `linv_one`: each block is lower triangular with a positive diagonal. `sigma_root`: symmetric. `linv_two`: each block is lower triangular with a positive diagonal.
All inputs are finite; a program needn't handle non-finite values. No bound on the sum of `mask_one` or of `mask_two` on one device may be relied on, other than what follows from the above.
Results may differ from a plain program's by a relative error of at most 0.00045.
Values may be sent and summed in bfloat16 or wider, within the bound.
No kernel may reach another device: no remote copies, remote signals or barrier semaphores. Data moves between devices by JAX's collectives and lax.ppermute only.
A program may use at most 64 MiB of HBM per device.

v0:
```python
import jax
import jax.numpy as jnp
from jax import lax
from jax.sharding import PartitionSpec as P

TILE = 128


def pattern_rows(tile_list):
    offsets = jnp.arange(TILE, dtype=jnp.int32)
    return (tile_list[..., None] * TILE + offsets).reshape(tile_list.shape[:-1] + (-1,))


def expand_mask(tile_mask):
    return jnp.repeat(jnp.repeat(tile_mask, TILE, axis=0), TILE, axis=1)


def assemble(selected, row_list):
    gathered = lax.all_gather(selected, "row", axis=1, tiled=True)
    return jnp.take(gathered, row_list, axis=1)


def solve_block(selected, row_list, linv_local, panel_local, mask_local):
    select = assemble(selected, row_list)
    masked = panel_local * expand_mask(mask_local).astype(jnp.bfloat16)
    linv_wide = linv_local.astype(jnp.float32)
    whole_panel = lax.all_gather(masked, "row", axis=1, tiled=True)
    upper_part = jnp.dot(whole_panel, linv_local, preferred_element_type=jnp.float32)
    cross = -jnp.dot(select, upper_part, precision=lax.Precision.HIGHEST)
    middle = linv_wide - jnp.dot(
        whole_panel.astype(jnp.float32).T, cross, precision=lax.Precision.HIGHEST
    )
    sigma = jnp.dot(
        lax.all_gather(linv_local, "row", axis=1, tiled=True).astype(jnp.float32).T,
        middle,
        precision=lax.Precision.HIGHEST,
    )
    return (sigma, cross)


def body(
    sigma_root,
    linv_one,
    panel_one,
    tiles_one,
    mask_one,
    linv_two,
    panel_two,
    tiles_two,
    mask_two,
    parent,
):
    leaf_id = lax.axis_index("leaf")
    width = sigma_root.shape[1]
    own_tiles = lax.dynamic_index_in_dim(tiles_one, leaf_id, 0, keepdims=False)
    rows_first = pattern_rows(own_tiles)
    selected_first = jnp.take(sigma_root, rows_first, axis=0)
    sigma_first, cross_first = solve_block(
        selected_first, rows_first, linv_one[0], panel_one[0], mask_one[0]
    )
    rows_every = pattern_rows(tiles_two)
    count = rows_every.shape[0]
    block_rows = rows_every.shape[1]
    owned = (parent == leaf_id).astype(jnp.float32)
    slots = jnp.take(sigma_first, rows_every.reshape(-1), axis=0).reshape(count, block_rows, width)
    slots = slots * owned[:, None, None]
    arrived = lax.all_to_all(slots, "leaf", split_axis=0, concat_axis=0, tiled=True)
    selected_second = jnp.sum(arrived, axis=0)
    rows_second = lax.dynamic_index_in_dim(rows_every, leaf_id, 0, keepdims=False)
    sigma_second, cross_second = solve_block(
        selected_second, rows_second, linv_two[0], panel_two[0], mask_two[0]
    )
    return (sigma_first[None], cross_first[None], sigma_second[None], cross_second[None])


def solution(mesh):
    return jax.shard_map(
        body,
        mesh=mesh,
        in_specs=(
            P(None, "row"),
            P("leaf", None, "row"),
            P("leaf", None, "row"),
            P(),
            P("leaf", None, "row"),
            P("leaf", None, "row"),
            P("leaf", None, "row"),
            P(),
            P("leaf", None, "row"),
            P(),
        ),
        out_specs=(
            P("leaf", None, "row"),
            P("leaf", None, "row"),
            P("leaf", None, "row"),
            P("leaf", None, "row"),
        ),
        check_vma=False,
    )
```

profile of v0, /device:TPU:1, one launch (start us, length us, event | category | flops | bytes accessed | tf_op | source)
XLA Modules:
  0.0 404.3 jit_solution(16791441184361963141)
XLA Ops:
  8.1 1.7 bitcast_multiply_fusion.1
  16.1 39.5 %all-gather.9.cloned.1.call-done = bf16[512,2048]{1,0:T(8,128)(2,1)} async-done(((bf16[512,128]{1,0:T(8,128)(2,1)}), bf16[512,2048]{1,0:T(8,128)(2,1)}) %all-gather.9.cloned.1.call-update) | async-done | bytes 2097168 | tf_op jit(solution)/shard_map/all_gather | solution.py:27
  55.5 2.3 fusion.13
  57.8 48.6 %all-gather.11.cloned.1.call-done = f32[512,2048]{1,0:T(8,128)} async-done(((f32[512,128]{1,0:T(8,128)}), f32[512,2048]{1,0:T(8,128)}) %all-gather.11.cloned.1.call-update) | async-done | bytes 4194320 | tf_op jit(solution)/shard_map/all_gather | solution.py:19
  106.5 5.3 %copy.19 = f32[512,2048]{0,1:T(8,128)} copy(f32[512,2048]{1,0:T(8,128)} %all-gather.11.cloned.1.call-done) | data formatting | bytes 8388608 | tf_op jit(solution)/shard_map/all_gather | solution.py:19
  111.8 4.2 %gather_fusion.2 = f32[512,512]{1,0:T(8,128)S(1)} fusion(f32[512,2048]{0,1:T(8,128)} %copy.19, s32[1024]{0:T(1024)S(1)} %pad_clamp_fusion.1), kind=kCustom, calls=%fused_computation.clone | custom fusion | bytes 2099200 | tf_op jit(solution)/shard_map/jit(_take)/gather | solution.py:20
  116.0 1.9 convolution_negate_fusion.1
  118.6 3.9 convolution_subtract_fusion.1
  122.6 50.3 %all-gather.17.cloned.1.call-done = bf16[1,2048,2048]{2,1,0:T(8,128)(2,1)} async-done(((bf16[1,2048,128]{2,1,0:T(8,128)(2,1)}), bf16[1,2048,2048]{2,1,0:T(8,128)(2,1)}) %all-gather.17.cloned.1.call-update) | async-done | bytes 8388624 | tf_op jit(solution)/shard_map/all_gather | solution.py:34
  172.9 6.3 %fusion.2 = f32[128,2048]{1,0:T(8,128)S(1)} fusion(f32[2048,128]{1,0:T(8,128)S(1)} %convolution_subtract_fusion.1, bf16[1,2048,2048]{2,1,0:T(8,128)(2,1)} %all-gather.17.cloned.1.call-done), kind=kOutput, calls=%fused_computation.6 | convolution fusion | flops 6442450944 | bytes 10485760 | tf_op jit(solution)/shard_map/dot_general | solution.py:33
  179.5 27.8 %gather_fusion.1 = f32[8192,128]{1,0:T(8,128)} fusion(f32[2048,128]{1,0:T(8,128)S(1)} %copy.21, s32[8192]{0:T(1024)S(1)} %broadcast_clamp_fusion), kind=kCustom, calls=%fused_computation.3 | custom fusion | bytes 8421376 | tf_op jit(solution)/shard_map/jit(_take)/gather | solution.py:65
  207.3 5.3 %select_multiply_fusion = f32[16,512,128]{2,1,0:T(8,128)} fusion(f32[16,512,128]{2,1,0:T(8,128)} %bitcast.84, f32[16]{0:T(128)S(1)} %compare_convert_fusion, pred[16,512]{1,0:T(8,128)(4,1)S(1)} %compare_and_fusion), kind=kLoop, calls=%fused_computation.8 | loop fusion | flops 2097152 | bytes 8396864 | tf_op jit(solution)/shard_map/mul | solution.py:66
  212.5 4.7 %all-to-all-start = ((f32[16,512,128]{2,1,0:T(8,128)}), f32[16,512,128]{2,1,0:T(8,128)}, u32[]{:S(2)}, u32[]{:S(2)}) async-start(f32[16,512,128]{2,1,0:T(8,128)} %select_multiply_fusion), calls=%async_computation | async-start | bytes 8388608 | tf_op jit(solution)/shard_map/all_to_all | solution.py:67
  218.2 62.3 %all-to-all-done = f32[16,512,128]{2,1,0:T(8,128)} async-done(((f32[16,512,128]{2,1,0:T(8,128)}), f32[16,512,128]{2,1,0:T(8,128)}, u32[]{:S(2)}, u32[]{:S(2)}) %all-to-all-start) | async-done | bytes 4194336 | tf_op jit(solution)/shard_map/all_to_all | solution.py:67
  280.5 2.4 reduce_sum.9
  284.4 2.3 fusion.11
  286.7 1.3 copy.23
  288.0 35.5 %all-gather.15.cloned.1.call-done = f32[512,2048]{0,1:T(8,128)} async-done(((f32[512,128]{0,1:T(8,128)}), f32[512,2048]{0,1:T(8,128)}) %all-gather.15.cloned.1.call-update) | async-done | bytes 4194320 | tf_op jit(solution)/shard_map/all_gather | solution.py:19
  323.6 4.2 %gather_fusion.3 = f32[512,512]{1,0:T(8,128)S(1)} fusion(f32[512,2048]{0,1:T(8,128)} %all-gather.15.cloned.1.call-done, s32[1024]{0:T(1024)S(1)} %pad_clamp_fusion), kind=kCustom, calls=%fused_computation.1.clone | custom fusion | bytes 2099200 | tf_op jit(solution)/shard_map/jit(_take)/gather | solution.py:20
  327.8 1.9 convolution_negate_fusion
  329.7 4.0 convolution_subtract_fusion
  333.7 56.2 %all-gather.19.cloned.1.call-done = bf16[1,2048,2048]{2,1,0:T(8,128)(2,1)} async-done(((bf16[1,2048,128]{2,1,0:T(8,128)(2,1)}), bf16[1,2048,2048]{2,1,0:T(8,128)(2,1)}) %all-gather.19.cloned.1.call-update) | async-done | bytes 8388624 | tf_op jit(solution)/shard_map/all_gather | solution.py:34
  389.9 6.3 %fusion.4 = f32[1,2048,128]{1,2,0:T(8,128)S(1)} fusion(f32[2048,128]{1,0:T(8,128)S(1)} %convolution_subtract_fusion, bf16[1,2048,2048]{2,1,0:T(8,128)(2,1)} %all-gather.19.cloned.1.call-done), kind=kOutput, calls=%fused_computation.9 | convolution fusion | flops 6442450944 | bytes 10485760 | tf_op jit(solution)/shard_map/dot_general | solution.py:33
  396.2 1.3 copy.24
  (58 shorter events, 10.5 us)
Async XLA Ops:
  7.2 3.6 copy-start
  7.2 48.4 %copy-start.1 = (bf16[1,2048,128]{2,1,0:T(8,128)(2,1)S(1)}, bf16[1,2048,128]{2,1,0:T(8,128)(2,1)}, u32[]{:S(2)}) copy-start(bf16[1,2048,128]{2,1,0:T(8,128)(2,1)} %param.13) | copy-start | bytes 1572868
  7.2 48.3 %all-gather.9.cloned.1.call-start = ((), (), s32[]{:S(2)}) async-start(), calls=%async_computation.1 | async-start | bytes 2228224 | tf_op jit(solution)/shard_map/all_gather | solution.py:27
  9.8 96.7 %all-gather.11.cloned.1.call-start = ((), (), s32[]{:S(2)}) async-start(), calls=%async_computation.2 | async-start | bytes 4456448 | tf_op jit(solution)/shard_map/all_gather | solution.py:19
  12.8 160.1 %all-gather.17.cloned.1.call-start = ((), (), s32[]{:S(2)}) async-start(), calls=%async_computation.5 | async-start | bytes 8912896 | tf_op jit(solution)/shard_map/all_gather | solution.py:34
  117.9 0.7 copy-start.4
  212.5 4.8 %copy-start.6 = (bf16[1,512,128]{2,1,0:T(8,128)(2,1)S(1)}, bf16[1,512,128]{2,1,0:T(8,128)(2,1)}, u32[]{:S(2)}) copy-start(bf16[1,512,128]{2,1,0:T(8,128)(2,1)} %param.18) | copy-start | bytes 393220
  212.5 67.9 %all-to-all-start = ((f32[16,512,128]{2,1,0:T(8,128)}), f32[16,512,128]{2,1,0:T(8,128)}, u32[]{:S(2)}, u32[]{:S(2)}) async-start(f32[16,512,128]{2,1,0:T(8,128)} %select_multiply_fusion), calls=%async_computation | async-start | bytes 8388608 | tf_op jit(solution)/shard_map/all_to_all | solution.py:67
  217.2 67.2 %copy-start.2 = (bf16[1,2048,128]{2,1,0:T(8,128)(2,1)S(1)}, bf16[1,2048,128]{2,1,0:T(8,128)(2,1)}, u32[]{:S(2)}) copy-start(bf16[1,2048,128]{2,1,0:T(8,128)(2,1)} %param.17) | copy-start | bytes 1572868
  217.2 67.2 %all-gather.13.cloned.1.call-start = ((), (), s32[]{:S(2)}) async-start(), calls=%async_computation.3 | async-start | bytes 2228224 | tf_op jit(solution)/shard_map/all_gather | solution.py:27
  218.1 105.4 %all-gather.15.cloned.1.call-start = ((), (), s32[]{:S(2)}) async-start(), calls=%async_computation.4 | async-start | bytes 4456448 | tf_op jit(solution)/shard_map/all_gather | solution.py:19
  283.7 106.2 %all-gather.19.cloned.1.call-start = ((), (), s32[]{:S(2)}) async-start(), calls=%async_computation.6 | async-start | bytes 8912896 | tf_op jit(solution)/shard_map/all_gather | solution.py:34
  288.0 41.6 %copy-start.3 = (bf16[1,2048,128]{2,1,0:T(8,128)(2,1)S(1)}, bf16[1,2048,128]{2,1,0:T(8,128)(2,1)}, u32[]{:S(2)}) copy-start(bf16[1,2048,128]{2,1,0:T(8,128)(2,1)} %param.17) | copy-start | bytes 1572868
  329.7 4.0 copy-start.5
Sparse Core Ops, SparseCore 0:
  10.4 45.1 all-gather.8
  57.9 48.5 all-gather.10
  108.2 64.6 all-gather.16
  220.1 40.0 all-gather.12
  283.9 39.6 all-gather.14
  325.2 64.6 all-gather.18
where the time goes:
time: 405 us; the launch traced here: 404 us
  waiting for transfers between devices  294 us (73%)
  local copies, waits for them, and re-layouts  47.4 us (12%)
  matrix products  28.8 us (7%)
  other arithmetic  15.1 us (4%)
  between operations  14.4 us (4%)
  starting transfers between devices  5.12 us (1%)
    all_gather x2, waiting for transfers between devices, solve_block(): lax.all_gather(linv_local, 'row', axis=1, tiled=True).astype(jnp.float32)  107 us
    all_gather x2, waiting for transfers between devices, assemble(): gathered = lax.all_gather(selected, 'row', axis=1, tiled=True)  84.1 us
    all_to_all x1, waiting for transfers between devices, body(): lax.all_to_all(slots, 'leaf', split_axis=0, concat_axis=0, tiled=True)  62.3 us
    all_gather x2, waiting for transfers between devices, solve_block(): whole_panel = lax.all_gather(masked, 'row', axis=1, tiled=True)  39.5 us
    gather x1, local copies, waits for them, and re-layouts, body(): jnp.take(sigma_first, rows_every.reshape(-1), axis=0)  27.8 us
    dot_general x2, matrix products, solve_block(): jnp.dot(lax.all_gather(linv_local, 'row', axis=1, tiled=True).astype(jnp....  12.5 us
    gather x2, local copies, waits for them, and re-layouts, assemble(): return jnp.take(gathered, row_list, axis=1)  8.43 us
  transfers between devices with their start and end apart: 7, of which 6 were waited for; matrix products, arithmetic and copies ran while one was open for 10% of the time, Pallas kernels for 0%

commit v1 on v0

--- a/solution.py
+++ b/solution.py
@@ -4,6 +4,16 @@
 from jax.sharding import PartitionSpec as P
 
 TILE = 128
+
+
+def pass_along(x, axis, d):
+    size = lax.axis_size(axis)
+    moving, parts = (x, [x])
+    for _ in range(size - 1):
+        moving = lax.ppermute(moving, axis, [(i, (i + 1) % size) for i in range(size)])
+        parts.insert(0, moving)
+    line = jnp.concatenate(parts, axis=d)
+    return jnp.roll(line, (lax.axis_index(axis) + 1) * x.shape[d], axis=d)
 
 
 def pattern_rows(tile_list):
@@ -24,7 +34,7 @@
     select = assemble(selected, row_list)
     masked = panel_local * expand_mask(mask_local).astype(jnp.bfloat16)
     linv_wide = linv_local.astype(jnp.float32)
-    whole_panel = lax.all_gather(masked, "row", axis=1, tiled=True)
+    whole_panel = pass_along(masked, "row", 1)
     upper_part = jnp.dot(whole_panel, linv_local, preferred_element_type=jnp.float32)
     cross = -jnp.dot(select, upper_part, precision=lax.Precision.HIGHEST)
     middle = linv_wide - jnp.dot(

time: 405 us -> 374 us (0.923)
  waiting for transfers between devices: 294 us -> 189 us
  blocking collectives: 0 us -> 56.9 us
  starting transfers between devices: 5.12 us -> 22.3 us
  other arithmetic: 15.1 us -> 8.87 us
    ppermute x0 -> x30, waiting for transfers between devices: none -> 179 us  [pass_along(): lax.ppermute(moving, axis, [(i, (i + 1) % size) for i in range(size)])]
    all_gather x2, waiting for transfers between devices: 107 us -> 8.76 us  [solve_block(): lax.all_gather(linv_local, 'row', axis=1, tiled=True).astype(jnp.float32)]
    all_gather x2, waiting for transfers between devices: 84.1 us -> 0.02 us  [assemble(): gathered = lax.all_gather(selected, 'row', axis=1, tiled=True)]
    all_to_all x1 -> x0, waiting for transfers between devices: 62.3 us -> none  [body(): lax.all_to_all(slots, 'leaf', split_axis=0, concat_axis=0, tiled=True)]
    all_to_all x0 -> x1, blocking collectives: none -> 56.9 us  [body(): lax.all_to_all(slots, 'leaf', split_axis=0, concat_axis=0, tiled=True)]
    all_gather x2 -> x0, waiting for transfers between devices: 39.5 us -> none  [solve_block(): whole_panel = lax.all_gather(masked, 'row', axis=1, tiled=True)]
    ppermute x0 -> x30, starting transfers between devices: none -> 22.2 us  [pass_along(): lax.ppermute(moving, axis, [(i, (i + 1) % size) for i in range(size)])]
    all_to_all x1 -> x0, starting transfers between devices: 4.69 us -> none  [body(): lax.all_to_all(slots, 'leaf', split_axis=0, concat_axis=0, tiled=True)]
  transfers between devices with their start and end apart: 7 -> 34, of which waited for: 6 -> 31; matrix products, arithmetic and copies ran while one was open for 10% -> 9% of each run, Pallas kernels for 0% -> 0%
where the time goes in v1:
time: 374 us; the launch traced here: 371 us
  waiting for transfers between devices  189 us (51%)
  blocking collectives  56.9 us (15%)
  local copies, waits for them, and re-layouts  51.4 us (14%)
  matrix products  28.2 us (8%)
  starting transfers between devices  22.3 us (6%)
  between operations  14.4 us (4%)
  other arithmetic  8.87 us (2%)
    ppermute x30, waiting for transfers between devices, pass_along(): lax.ppermute(moving, axis, [(i, (i + 1) % size) for i in range(size)])  179 us
    all_to_all x1, blocking collectives, body(): lax.all_to_all(slots, 'leaf', split_axis=0, concat_axis=0, tiled=True)  56.9 us
    gather x1, local copies, waits for them, and re-layouts, body(): jnp.take(sigma_first, rows_every.reshape(-1), axis=0)  27.9 us
    ppermute x30, starting transfers between devices, pass_along(): lax.ppermute(moving, axis, [(i, (i + 1) % size) for i in range(size)])  22.2 us
    dot_general x2, matrix products, solve_block(): jnp.dot(lax.all_gather(linv_local, 'row', axis=1, tiled=True).astype(jnp....  12.5 us
    all_gather x2, waiting for transfers between devices, solve_block(): lax.all_gather(linv_local, 'row', axis=1, tiled=True).astype(jnp.float32)  8.76 us
    dot_general x2, matrix products, solve_block(): jnp.dot(whole_panel.astype(jnp.float32).T, cross, precision=lax.Precision...  8.71 us
    gather x2, local copies, waits for them, and re-layouts, assemble(): return jnp.take(gathered, row_list, axis=1)  8.57 us
  transfers between devices with their start and end apart: 34, of which 31 were waited for; matrix products, arithmetic and copies ran while one was open for 9% of the time, Pallas kernels for 0%

profile of v1, /device:TPU:1, one launch (start us, length us, event | category | flops | bytes accessed | tf_op | source)
XLA Modules:
  0.0 370.6 jit_solution(10214467699892546171)
XLA Ops:
  27.6 7.3 %collective-permute-done.3 = bf16[512,128]{1,0:T(8,128)(2,1)S(1)} collective-permute-done((bf16[512,128]{1,0:T(8,128)(2,1)S(1)}, bf16[512,128]{1,0:T(8,128)(2,1)S(1)}, u32[]{:S(2)}, u32[]{:S(2)}) %collective-permute-start.3) | collective-permute-done | bytes 131104 | tf_op jit(solution)/shard_map/ppermute | solution.py:13
  34.9 6.1 %collective-permute-done.4 = bf16[512,128]{1,0:T(8,128)(2,1)S(1)} collective-permute-done((bf16[512,128]{1,0:T(8,128)(2,1)S(1)}, bf16[512,128]{1,0:T(8,128)(2,1)S(1)}, u32[]{:S(2)}, u32[]{:S(2)}) %collective-permute-start.4) | collective-permute-done | bytes 131104 | tf_op jit(solution)/shard_map/ppermute | solution.py:13
  41.0 5.7 %collective-permute-done.5 = bf16[512,128]{1,0:T(8,128)(2,1)S(1)} collective-permute-done((bf16[512,128]{1,0:T(8,128)(2,1)S(1)}, bf16[512,128]{1,0:T(8,128)(2,1)S(1)}, u32[]{:S(2)}, u32[]{:S(2)}) %collective-permute-start.5) | collective-permute-done | bytes 131104 | tf_op jit(solution)/shard_map/ppermute | solution.py:13
  46.7 6.8 %collective-permute-done.6 = bf16[512,128]{1,0:T(8,128)(2,1)S(1)} collective-permute-done((bf16[512,128]{1,0:T(8,128)(2,1)S(1)}, bf16[512,128]{1,0:T(8,128)(2,1)S(1)}, u32[]{:S(2)}, u32[]{:S(2)}) %collective-permute-start.6) | collective-permute-done | bytes 131104 | tf_op jit(solution)/shard_map/ppermute | solution.py:13
  53.5 6.2 %collective-permute-done.7 = bf16[512,128]{1,0:T(8,128)(2,1)S(1)} collective-permute-done((bf16[512,128]{1,0:T(8,128)(2,1)S(1)}, bf16[512,128]{1,0:T(8,128)(2,1)S(1)}, u32[]{:S(2)}, u32[]{:S(2)}) %collective-permute-start.7) | collective-permute-done | bytes 131104 | tf_op jit(solution)/shard_map/ppermute | solution.py:13
  60.2 6.0 %collective-permute-done.8 = bf16[512,128]{1,0:T(8,128)(2,1)S(1)} collective-permute-done((bf16[512,128]{1,0:T(8,128)(2,1)S(1)}, bf16[512,128]{1,0:T(8,128)(2,1)S(1)}, u32[]{:S(2)}, u32[]{:S(2)}) %collective-permute-start.8) | collective-permute-done | bytes 131104 | tf_op jit(solution)/shard_map/ppermute | solution.py:13
  83.0 8.3 %collective-permute-done.12 = bf16[512,128]{1,0:T(8,128)(2,1)S(1)} collective-permute-done((bf16[512,128]{1,0:T(8,128)(2,1)S(1)}, bf16[512,128]{1,0:T(8,128)(2,1)S(1)}, u32[]{:S(2)}, u32[]{:S(2)}) %collective-permute-start.12) | collective-permute-done | bytes 131104 | tf_op jit(solution)/shard_map/ppermute | solution.py:13
  91.4 8.2 %collective-permute-done.13 = bf16[512,128]{1,0:T(8,128)(2,1)} collective-permute-done((bf16[512,128]{1,0:T(8,128)(2,1)S(1)}, bf16[512,128]{1,0:T(8,128)(2,1)}, u32[]{:S(2)}, u32[]{:S(2)}) %collective-permute-start.13) | collective-permute-done | bytes 131104 | tf_op jit(solution)/shard_map/ppermute | solution.py:13
  99.7 8.5 %collective-permute-done.14 = bf16[512,128]{1,0:T(8,128)(2,1)} collective-permute-done((bf16[512,128]{1,0:T(8,128)(2,1)}, bf16[512,128]{1,0:T(8,128)(2,1)}, u32[]{:S(2)}, u32[]{:S(2)}) %collective-permute-start.14) | collective-permute-done | bytes 131104 | tf_op jit(solution)/shard_map/ppermute | solution.py:13
  129.3 8.7 %all-gather.11.cloned.1.call-done = bf16[1,2048,2048]{2,1,0:T(8,128)(2,1)} async-done(((bf16[1,2048,128]{2,1,0:T(8,128)(2,1)}), bf16[1,2048,2048]{2,1,0:T(8,128)(2,1)}) %all-gather.11.cloned.1.call-update) | async-done | bytes 8388624 | tf_op jit(solution)/shard_map/all_gather | solution.py:44
  138.0 6.3 %fusion.2 = f32[128,2048]{1,0:T(8,128)S(1)} fusion(f32[2048,128]{1,0:T(8,128)S(1)} %convolution_subtract_fusion.1, bf16[1,2048,2048]{2,1,0:T(8,128)(2,1)} %all-gather.11.cloned.1.call-done), kind=kOutput, calls=%fused_computation.6 | convolution fusion | flops 6442450944 | bytes 10485760 | tf_op jit(solution)/shard_map/dot_general | solution.py:43
  144.6 27.9 %gather_fusion.1 = f32[8192,128]{1,0:T(8,128)} fusion(f32[2048,128]{1,0:T(8,128)S(1)} %copy.21, s32[8192]{0:T(1024)S(1)} %broadcast_clamp_fusion), kind=kCustom, calls=%fused_computation.3 | custom fusion | bytes 8421376 | tf_op jit(solution)/shard_map/jit(_take)/gather | solution.py:75
  176.1 56.9 %all_to_all.5 = f32[16,512,128]{2,1,0:T(8,128)} all-to-all(f32[16,512,128]{2,1,0:T(8,128)S(1)} %select_multiply_fusion), channel_id=1, replica_groups=mesh['leaf'=16,'row'=16] {'leaf'}, dimensions={0} | all-to-all | bytes 8388608 | tf_op jit(solution)/shard_map/all_to_all | solution.py:77
  270.2 6.0 %collective-permute-done.20 = bf16[512,128]{1,0:T(8,128)(2,1)S(1)} collective-permute-done((bf16[512,128]{1,0:T(8,128)(2,1)S(1)}, bf16[512,128]{1,0:T(8,128)(2,1)S(1)}, u32[]{:S(2)}, u32[]{:S(2)}) %collective-permute-start.20) | collective-permute-done | bytes 131104 | tf_op jit(solution)/shard_map/ppermute | solution.py:13
  276.2 5.6 %collective-permute-done.21 = bf16[512,128]{1,0:T(8,128)(2,1)S(1)} collective-permute-done((bf16[512,128]{1,0:T(8,128)(2,1)S(1)}, bf16[512,128]{1,0:T(8,128)(2,1)S(1)}, u32[]{:S(2)}, u32[]{:S(2)}) %collective-permute-start.21) | collective-permute-done | bytes 131104 | tf_op jit(solution)/shard_map/ppermute | solution.py:13
  281.8 5.6 %collective-permute-done.22 = bf16[512,128]{1,0:T(8,128)(2,1)S(1)} collective-permute-done((bf16[512,128]{1,0:T(8,128)(2,1)S(1)}, bf16[512,128]{1,0:T(8,128)(2,1)S(1)}, u32[]{:S(2)}, u32[]{:S(2)}) %collective-permute-start.22) | collective-permute-done | bytes 131104 | tf_op jit(solution)/shard_map/ppermute | solution.py:13
  287.4 5.6 %collective-permute-done.23 = bf16[512,128]{1,0:T(8,128)(2,1)S(1)} collective-permute-done((bf16[512,128]{1,0:T(8,128)(2,1)S(1)}, bf16[512,128]{1,0:T(8,128)(2,1)S(1)}, u32[]{:S(2)}, u32[]{:S(2)}) %collective-permute-start.23) | collective-permute-done | bytes 131104 | tf_op jit(solution)/shard_map/ppermute | solution.py:13
  293.3 7.4 %collective-permute-done.24 = bf16[512,128]{1,0:T(8,128)(2,1)S(1)} collective-permute-done((bf16[512,128]{1,0:T(8,128)(2,1)S(1)}, bf16[512,128]{1,0:T(8,128)(2,1)S(1)}, u32[]{:S(2)}, u32[]{:S(2)}) %collective-permute-start.24) | collective-permute-done | bytes 131104 | tf_op jit(solution)/shard_map/ppermute | solution.py:13
  300.7 8.2 %collective-permute-done.25 = bf16[512,128]{1,0:T(8,128)(2,1)S(1)} collective-permute-done((bf16[512,128]{1,0:T(8,128)(2,1)S(1)}, bf16[512,128]{1,0:T(8,128)(2,1)S(1)}, u32[]{:S(2)}, u32[]{:S(2)}) %collective-permute-start.25) | collective-permute-done | bytes 131104 | tf_op jit(solution)/shard_map/ppermute | solution.py:13
  309.0 8.2 %collective-permute-done.26 = bf16[512,128]{1,0:T(8,128)(2,1)S(1)} collective-permute-done((bf16[512,128]{1,0:T(8,128)(2,1)S(1)}, bf16[512,128]{1,0:T(8,128)(2,1)S(1)}, u32[]{:S(2)}, u32[]{:S(2)}) %collective-permute-start.26) | collective-permute-done | bytes 131104 | tf_op jit(solution)/shard_map/ppermute | solution.py:13
  317.2 8.3 %collective-permute-done.27 = bf16[512,128]{1,0:T(8,128)(2,1)S(1)} collective-permute-done((bf16[512,128]{1,0:T(8,128)(2,1)S(1)}, bf16[512,128]{1,0:T(8,128)(2,1)S(1)}, u32[]{:S(2)}, u32[]{:S(2)}) %collective-permute-start.27) | collective-permute-done | bytes 131104 | tf_op jit(solution)/shard_map/ppermute | solution.py:13
  325.5 8.0 %collective-permute-done.28 = bf16[512,128]{1,0:T(8,128)(2,1)S(1)} collective-permute-done((bf16[512,128]{1,0:T(8,128)(2,1)S(1)}, bf16[512,128]{1,0:T(8,128)(2,1)S(1)}, u32[]{:S(2)}, u32[]{:S(2)}) %collective-permute-start.28) | collective-permute-done | bytes 131104 | tf_op jit(solution)/shard_map/ppermute | solution.py:13
  333.6 8.1 %collective-permute-done.29 = bf16[512,128]{1,0:T(8,128)(2,1)S(1)} collective-permute-done((bf16[512,128]{1,0:T(8,128)(2,1)S(1)}, bf16[512,128]{1,0:T(8,128)(2,1)S(1)}, u32[]{:S(2)}, u32[]{:S(2)}) %collective-permute-start.29) | collective-permute-done | bytes 131104 | tf_op jit(solution)/shard_map/ppermute | solution.py:13
  356.5 6.3 %fusion.4 = f32[1,2048,128]{1,2,0:T(8,128)S(1)} fusion(f32[2048,128]{1,0:T(8,128)S(1)} %convolution_subtract_fusion, bf16[1,2048,2048]{2,1,0:T(8,128)(2,1)} %all-gather.13.cloned.1.call-done), kind=kOutput, calls=%fused_computation.13 | convolution fusion | flops 6442450944 | bytes 10485760 | tf_op jit(solution)/shard_map/dot_general | solution.py:43
  (157 shorter events, 116.1 us)
Async XLA Ops:
  7.2 106.2 %all-gather.7.cloned.1.call-start = ((), (), s32[]{:S(2)}) async-start(), calls=%async_computation.1 | async-start | bytes 4456448 | tf_op jit(solution)/shard_map/all_gather | solution.py:29
  10.3 127.7 %all-gather.11.cloned.1.call-start = ((), (), s32[]{:S(2)}) async-start(), calls=%async_computation.3 | async-start | bytes 8912896 | tf_op jit(solution)/shard_map/all_gather | solution.py:44
  11.1 334.7 %all-gather.9.cloned.1.call-start = ((), (), s32[]{:S(2)}) async-start(), calls=%async_computation.2 | async-start | bytes 4456448 | tf_op jit(solution)/shard_map/all_gather | solution.py:29
  27.3 7.7 %collective-permute-start.3 = (bf16[512,128]{1,0:T(8,128)(2,1)S(1)}, bf16[512,128]{1,0:T(8,128)(2,1)S(1)}, u32[]{:S(2)}, u32[]{:S(2)}) collective-permute-start(bf16[512,128]{1,0:T(8,128)(2,1)S(1)} %collective-permute-done.2), channel_id=1, source_target_pairs={{0,1},{1,2},{2,3},{3,4},{4,5},{5,6},{6,7},{7,8},{8,9},{9,10},{10,1... | collective-permute-start | bytes 393224 | tf_op jit(solution)/shard_map/ppermute | solution.py:13
  34.9 6.1 %collective-permute-start.4 = (bf16[512,128]{1,0:T(8,128)(2,1)S(1)}, bf16[512,128]{1,0:T(8,128)(2,1)S(1)}, u32[]{:S(2)}, u32[]{:S(2)}) collective-permute-start(bf16[512,128]{1,0:T(8,128)(2,1)S(1)} %collective-permute-done.3), channel_id=1, source_target_pairs={{0,1},{1,2},{2,3},{3,4},{4,5},{5,6},{6,7},{7,8},{8,9},{9,10},{10,1... | collective-permute-start | bytes 393224 | tf_op jit(solution)/shard_map/ppermute | solution.py:13
  41.0 5.7 %collective-permute-start.5 = (bf16[512,128]{1,0:T(8,128)(2,1)S(1)}, bf16[512,128]{1,0:T(8,128)(2,1)S(1)}, u32[]{:S(2)}, u32[]{:S(2)}) collective-permute-start(bf16[512,128]{1,0:T(8,128)(2,1)S(1)} %collective-permute-done.4), channel_id=1, source_target_pairs={{0,1},{1,2},{2,3},{3,4},{4,5},{5,6},{6,7},{7,8},{8,9},{9,10},{10,1... | collective-permute-start | bytes 393224 | tf_op jit(solution)/shard_map/ppermute | solution.py:13
  46.7 6.8 %collective-permute-start.6 = (bf16[512,128]{1,0:T(8,128)(2,1)S(1)}, bf16[512,128]{1,0:T(8,128)(2,1)S(1)}, u32[]{:S(2)}, u32[]{:S(2)}) collective-permute-start(bf16[512,128]{1,0:T(8,128)(2,1)S(1)} %collective-permute-done.5), channel_id=1, source_target_pairs={{0,1},{1,2},{2,3},{3,4},{4,5},{5,6},{6,7},{7,8},{8,9},{9,10},{10,1... | collective-permute-start | bytes 393224 | tf_op jit(solution)/shard_map/ppermute | solution.py:13
  53.5 6.2 %collective-permute-start.7 = (bf16[512,128]{1,0:T(8,128)(2,1)S(1)}, bf16[512,128]{1,0:T(8,128)(2,1)S(1)}, u32[]{:S(2)}, u32[]{:S(2)}) collective-permute-start(bf16[512,128]{1,0:T(8,128)(2,1)S(1)} %collective-permute-done.6), channel_id=1, source_target_pairs={{0,1},{1,2},{2,3},{3,4},{4,5},{5,6},{6,7},{7,8},{8,9},{9,10},{10,1... | collective-permute-start | bytes 393224 | tf_op jit(solution)/shard_map/ppermute | solution.py:13
  59.6 6.6 %collective-permute-start.8 = (bf16[512,128]{1,0:T(8,128)(2,1)S(1)}, bf16[512,128]{1,0:T(8,128)(2,1)S(1)}, u32[]{:S(2)}, u32[]{:S(2)}) collective-permute-start(bf16[512,128]{1,0:T(8,128)(2,1)S(1)} %collective-permute-done.7), channel_id=1, source_target_pairs={{0,1},{1,2},{2,3},{3,4},{4,5},{5,6},{6,7},{7,8},{8,9},{9,10},{10,1... | collective-permute-start | bytes 393224 | tf_op jit(solution)/shard_map/ppermute | solution.py:13
  83.0 8.3 %collective-permute-start.12 = (bf16[512,128]{1,0:T(8,128)(2,1)S(1)}, bf16[512,128]{1,0:T(8,128)(2,1)S(1)}, u32[]{:S(2)}, u32[]{:S(2)}) collective-permute-start(bf16[512,128]{1,0:T(8,128)(2,1)S(1)} %collective-permute-done.11), channel_id=1, source_target_pairs={{0,1},{1,2},{2,3},{3,4},{4,5},{5,6},{6,7},{7,8},{8,9},{9,10},{10,1... | collective-permute-start | bytes 393224 | tf_op jit(solution)/shard_map/ppermute | solution.py:13
  91.3 8.3 %collective-permute-start.13 = (bf16[512,128]{1,0:T(8,128)(2,1)S(1)}, bf16[512,128]{1,0:T(8,128)(2,1)}, u32[]{:S(2)}, u32[]{:S(2)}) collective-permute-start(bf16[512,128]{1,0:T(8,128)(2,1)S(1)} %collective-permute-done.12), channel_id=1, source_target_pairs={{0,1},{1,2},{2,3},{3,4},{4,5},{5,6},{6,7},{7,8},{8,9},{9,10},{10,1... | collective-permute-start | bytes 393224 | tf_op jit(solution)/shard_map/ppermute | solution.py:13
  99.6 8.6 %collective-permute-start.14 = (bf16[512,128]{1,0:T(8,128)(2,1)}, bf16[512,128]{1,0:T(8,128)(2,1)}, u32[]{:S(2)}, u32[]{:S(2)}) collective-permute-start(bf16[512,128]{1,0:T(8,128)(2,1)} %collective-permute-done.13), channel_id=1, source_target_pairs={{0,1},{1,2},{2,3},{3,4},{4,5},{5,6},{6,7},{7,8},{8,9},{9,10},{10,1... | collective-permute-start | bytes 393224 | tf_op jit(solution)/shard_map/ppermute | solution.py:13
  236.3 120.2 %all-gather.13.cloned.1.call-start = ((), (), s32[]{:S(2)}) async-start(), calls=%async_computation.4 | async-start | bytes 8912896 | tf_op jit(solution)/shard_map/all_gather | solution.py:44
  242.4 6.1 %collective-permute-start.16 = (bf16[512,128]{1,0:T(8,128)(2,1)S(1)}, bf16[512,128]{1,0:T(8,128)(2,1)S(1)}, u32[]{:S(2)}, u32[]{:S(2)}) collective-permute-start(bf16[512,128]{1,0:T(8,128)(2,1)S(1)} %collective-permute-done.15), channel_id=1, source_target_pairs={{0,1},{1,2},{2,3},{3,4},{4,5},{5,6},{6,7},{7,8},{8,9},{9,10},{10,1... | collective-permute-start | bytes 393224 | tf_op jit(solution)/shard_map/ppermute | solution.py:13
  248.5 6.7 %collective-permute-start.17 = (bf16[512,128]{1,0:T(8,128)(2,1)S(1)}, bf16[512,128]{1,0:T(8,128)(2,1)S(1)}, u32[]{:S(2)}, u32[]{:S(2)}) collective-permute-start(bf16[512,128]{1,0:T(8,128)(2,1)S(1)} %collective-permute-done.16), channel_id=1, source_target_pairs={{0,1},{1,2},{2,3},{3,4},{4,5},{5,6},{6,7},{7,8},{8,9},{9,10},{10,1... | collective-permute-start | bytes 393224 | tf_op jit(solution)/shard_map/ppermute | solution.py:13
  255.2 6.7 %collective-permute-start.18 = (bf16[512,128]{1,0:T(8,128)(2,1)S(1)}, bf16[512,128]{1,0:T(8,128)(2,1)S(1)}, u32[]{:S(2)}, u32[]{:S(2)}) collective-permute-start(bf16[512,128]{1,0:T(8,128)(2,1)S(1)} %collective-permute-done.17), channel_id=1, source_target_pairs={{0,1},{1,2},{2,3},{3,4},{4,5},{5,6},{6,7},{7,8},{8,9},{9,10},{10,1... | collective-permute-start | bytes 393224 | tf_op jit(solution)/shard_map/ppermute | solution.py:13
  261.9 7.4 %collective-permute-start.19 = (bf16[512,128]{1,0:T(8,128)(2,1)S(1)}, bf16[512,128]{1,0:T(8,128)(2,1)S(1)}, u32[]{:S(2)}, u32[]{:S(2)}) collective-permute-start(bf16[512,128]{1,0:T(8,128)(2,1)S(1)} %collective-permute-done.18), channel_id=1, source_target_pairs={{0,1},{1,2},{2,3},{3,4},{4,5},{5,6},{6,7},{7,8},{8,9},{9,10},{10,1... | collective-permute-start | bytes 393224 | tf_op jit(solution)/shard_map/ppermute | solution.py:13
  269.3 6.9 %collective-permute-start.20 = (bf16[512,128]{1,0:T(8,128)(2,1)S(1)}, bf16[512,128]{1,0:T(8,128)(2,1)S(1)}, u32[]{:S(2)}, u32[]{:S(2)}) collective-permute-start(bf16[512,128]{1,0:T(8,128)(2,1)S(1)} %collective-permute-done.19), channel_id=1, source_target_pairs={{0,1},{1,2},{2,3},{3,4},{4,5},{5,6},{6,7},{7,8},{8,9},{9,10},{10,1... | collective-permute-start | bytes 393224 | tf_op jit(solution)/shard_map/ppermute | solution.py:13
  293.0 7.7 %collective-permute-start.24 = (bf16[512,128]{1,0:T(8,128)(2,1)S(1)}, bf16[512,128]{1,0:T(8,128)(2,1)S(1)}, u32[]{:S(2)}, u32[]{:S(2)}) collective-permute-start(bf16[512,128]{1,0:T(8,128)(2,1)S(1)} %collective-permute-done.23), channel_id=1, source_target_pairs={{0,1},{1,2},{2,3},{3,4},{4,5},{5,6},{6,7},{7,8},{8,9},{9,10},{10,1... | collective-permute-start | bytes 393224 | tf_op jit(solution)/shard_map/ppermute | solution.py:13
  300.7 8.2 %collective-permute-start.25 = (bf16[512,128]{1,0:T(8,128)(2,1)S(1)}, bf16[512,128]{1,0:T(8,128)(2,1)S(1)}, u32[]{:S(2)}, u32[]{:S(2)}) collective-permute-start(bf16[512,128]{1,0:T(8,128)(2,1)S(1)} %collective-permute-done.24), channel_id=1, source_target_pairs={{0,1},{1,2},{2,3},{3,4},{4,5},{5,6},{6,7},{7,8},{8,9},{9,10},{10,1... | collective-permute-start | bytes 393224 | tf_op jit(solution)/shard_map/ppermute | solution.py:13
  308.9 8.3 %collective-permute-start.26 = (bf16[512,128]{1,0:T(8,128)(2,1)S(1)}, bf16[512,128]{1,0:T(8,128)(2,1)S(1)}, u32[]{:S(2)}, u32[]{:S(2)}) collective-permute-start(bf16[512,128]{1,0:T(8,128)(2,1)S(1)} %collective-permute-done.25), channel_id=1, source_target_pairs={{0,1},{1,2},{2,3},{3,4},{4,5},{5,6},{6,7},{7,8},{8,9},{9,10},{10,1... | collective-permute-start | bytes 393224 | tf_op jit(solution)/shard_map/ppermute | solution.py:13
  317.2 8.3 %collective-permute-start.27 = (bf16[512,128]{1,0:T(8,128)(2,1)S(1)}, bf16[512,128]{1,0:T(8,128)(2,1)S(1)}, u32[]{:S(2)}, u32[]{:S(2)}) collective-permute-start(bf16[512,128]{1,0:T(8,128)(2,1)S(1)} %collective-permute-done.26), channel_id=1, source_target_pairs={{0,1},{1,2},{2,3},{3,4},{4,5},{5,6},{6,7},{7,8},{8,9},{9,10},{10,1... | collective-permute-start | bytes 393224 | tf_op jit(solution)/shard_map/ppermute | solution.py:13
  325.5 8.0 %collective-permute-start.28 = (bf16[512,128]{1,0:T(8,128)(2,1)S(1)}, bf16[512,128]{1,0:T(8,128)(2,1)S(1)}, u32[]{:S(2)}, u32[]{:S(2)}) collective-permute-start(bf16[512,128]{1,0:T(8,128)(2,1)S(1)} %collective-permute-done.27), channel_id=1, source_target_pairs={{0,1},{1,2},{2,3},{3,4},{4,5},{5,6},{6,7},{7,8},{8,9},{9,10},{10,1... | collective-permute-start | bytes 393224 | tf_op jit(solution)/shard_map/ppermute | solution.py:13
  333.5 8.1 %collective-permute-start.29 = (bf16[512,128]{1,0:T(8,128)(2,1)S(1)}, bf16[512,128]{1,0:T(8,128)(2,1)S(1)}, u32[]{:S(2)}, u32[]{:S(2)}) collective-permute-start(bf16[512,128]{1,0:T(8,128)(2,1)S(1)} %collective-permute-done.28), channel_id=1, source_target_pairs={{0,1},{1,2},{2,3},{3,4},{4,5},{5,6},{6,7},{7,8},{8,9},{9,10},{10,1... | collective-permute-start | bytes 393224 | tf_op jit(solution)/shard_map/ppermute | solution.py:13
  (24 other events, 253.9 us)
Sparse Core Ops, SparseCore 0:
  10.4 56.9 all-gather.6
  69.2 68.8 all-gather.10
  236.4 40.8 all-gather.8
  279.0 72.8 all-gather.12
